TPU v7x, 128 devices: a whole 4x4x4 slice. The times are simulated.
128 devices in a mesh: sample: 4 (over x_lo, core), freq: 32 (over y, z, x_hi).
Axes of the slice: x: 4 (x_hi: 2, x_lo: 2; x = x_hi * 2 + x_lo), y: 4, z: 4, core: 2. Of those that a mesh axis runs over, the one named last changes fastest.
Arguments:
- images: bfloat16 [1024, 32, 32, 128], P(('sample', 'freq')), may hold values from -6 to 6
- cotangent: bfloat16 [1024, 32, 32, 128], P(('sample', 'freq')), may hold values from -6 to 6
- kernel: float32 [3, 3, 128, 128], replicated, may hold values from -0.022097087 to 0.022097087
Outputs:
- outputs: bfloat16 [1024, 32, 32, 128], P(('sample', 'freq'))
- kernel_grad: float32 [3, 3, 128, 128], replicated
All inputs are finite; a program needn't handle non-finite values.
Results may differ from a plain program's by a relative error of at most 0.0064.
Values may be sent and summed in bfloat16 or wider, within the bound.
A program may use at most 128 MiB of HBM per device.

v0:
```python
import math

import jax
import jax.numpy as jnp
from jax import lax
from jax.sharding import PartitionSpec as P

NS_STEPS = 2


HIGHEST = lax.Precision.HIGHEST


def angle_tables(side_cells, half_cells):
    position = jnp.arange(side_cells, dtype=jnp.int32)
    columns = jnp.arange(half_cells, dtype=jnp.int32)
    across = position[:, None] * columns[None, :] % side_cells
    square = position[:, None] * position[None, :] % side_cells
    radians = 2.0 * math.pi / side_cells
    return (radians * across.astype(jnp.float32), radians * square.astype(jnp.float32))


def forward_spectrum(pictures, across_angle, square_angle):
    number = pictures.shape[0]
    side_cells = pictures.shape[1]
    channels = pictures.shape[3]
    half_cells = across_angle.shape[1]
    row_table = jnp.concatenate([jnp.cos(across_angle), -jnp.sin(across_angle)], axis=1)
    partial_sum = jnp.einsum(
        "nhwc,wk->nhkc", pictures, row_table, precision=HIGHEST, preferred_element_type=jnp.float32
    )
    partial_sum = partial_sum.reshape(number, side_cells, 2, half_cells, channels)
    cosine = jnp.cos(square_angle)
    sine_table = jnp.sin(square_angle)
    rotation = jnp.stack([jnp.stack([cosine, sine_table]), jnp.stack([-sine_table, cosine])])
    spectrum = jnp.einsum("abuh,nhbvc->nuvac", rotation, partial_sum, precision=HIGHEST)
    return spectrum.reshape(number, side_cells, half_cells, 2 * channels).astype(jnp.bfloat16)


def inverse_spectrum(spectrum, across_angle, square_angle):
    number = spectrum.shape[0]
    side_cells = spectrum.shape[1]
    half_cells = spectrum.shape[2]
    channels = spectrum.shape[3] // 2
    pieces = spectrum.reshape(number, side_cells, half_cells, 2, channels)
    cosine = jnp.cos(square_angle)
    sine_table = jnp.sin(square_angle)
    rotation = jnp.stack([jnp.stack([cosine, -sine_table]), jnp.stack([sine_table, cosine])])
    column_sum = jnp.einsum(
        "abuh,nuvbc->nhavc", rotation, pieces, precision=HIGHEST, preferred_element_type=jnp.float32
    )
    frequency = jnp.arange(half_cells, dtype=jnp.int32)
    boundary = (frequency == 0) | (frequency == side_cells // 2)
    weights = jnp.where(boundary, 1.0, 2.0).astype(jnp.float32) / (side_cells * side_cells)
    back_table = jnp.concatenate(
        [jnp.cos(across_angle).T * weights[:, None], -jnp.sin(across_angle).T * weights[:, None]],
        axis=0,
    )
    result = jnp.einsum(
        "nhkc,kw->nhwc",
        column_sum.reshape(number, side_cells, 2 * half_cells, channels),
        back_table,
        precision=HIGHEST,
    )
    return result.astype(jnp.bfloat16)


def tap_angles(row_numbers, side_cells, half_cells, tap_count):
    offsets = jnp.arange(tap_count, dtype=jnp.int32) - (tap_count - 1) // 2
    columns = jnp.arange(half_cells, dtype=jnp.int32)
    phases = (
        row_numbers[:, None, None, None] * offsets[None, None, :, None]
        + columns[None, :, None, None] * offsets[None, None, None, :]
    ) % side_cells
    phases = phases.reshape(row_numbers.shape[0] * half_cells, tap_count * tap_count)
    return 2.0 * math.pi / side_cells * phases.astype(jnp.float32)


def skew_matrix(kernel, angles):
    flattened = kernel.reshape(kernel.shape[0] * kernel.shape[1], kernel.shape[2], kernel.shape[3])
    real_part = jnp.einsum("ft,toi->foi", jnp.cos(angles), flattened, precision=HIGHEST)
    imag_part = -jnp.einsum("ft,toi->foi", jnp.sin(angles), flattened, precision=HIGHEST)
    return (real_part - jnp.swapaxes(real_part, 1, 2), imag_part + jnp.swapaxes(imag_part, 1, 2))


def low_multiply(former, latter):
    return jnp.einsum(
        "fij,fjk->fik",
        former.astype(jnp.bfloat16),
        latter.astype(jnp.bfloat16),
        preferred_element_type=jnp.float32,
    )


def full_multiply(former, latter):
    return jnp.einsum("fij,fjk->fik", former, latter, precision=HIGHEST)


def complex_product(former, latter, multiply):
    real_out = multiply(former[0], latter[0]) - multiply(former[1], latter[1])
    imag_out = multiply(former[0], latter[1]) + multiply(former[1], latter[0])
    return (real_out, imag_out)


def adjoint(matrix):
    return (jnp.swapaxes(matrix[0], 1, 2), -jnp.swapaxes(matrix[1], 1, 2))


def cayley_deviation(skew_part):
    deviation = (-skew_part[0], -skew_part[1])
    for iteration in range(NS_STEPS):
        cross_term = complex_product(skew_part, deviation, low_multiply)
        residue = (
            -(skew_part[0] + deviation[0] + cross_term[0]),
            -(skew_part[1] + deviation[1] + cross_term[1]),
        )
        update = complex_product(deviation, residue, low_multiply)
        deviation = (deviation[0] + residue[0] + update[0], deviation[1] + residue[1] + update[1])
    return deviation


def embedded(deviation):
    doubled_real = (2.0 * deviation[0]).astype(jnp.bfloat16)
    doubled_imag = (2.0 * deviation[1]).astype(jnp.bfloat16)
    upper_half = jnp.concatenate([doubled_real, -doubled_imag], axis=2)
    lower_half = jnp.concatenate([doubled_imag, doubled_real], axis=2)
    return jnp.concatenate([upper_half, lower_half], axis=1)


def grad_factor(side_cells, half_cells, total_images):
    frequency = jnp.arange(half_cells, dtype=jnp.int32)
    boundary = (frequency == 0) | (frequency == side_cells // 2)
    return jnp.where(boundary, 2.0, 4.0).astype(jnp.float32) / (
        side_cells * side_cells * total_images
    )


def skew_gradient(spec_grad, deviation):
    conjugate = adjoint(deviation)
    partial_term = complex_product(spec_grad, conjugate, full_multiply)
    partial_term = (spec_grad[0] + partial_term[0], spec_grad[1] + partial_term[1])
    outer_term = complex_product(conjugate, partial_term, full_multiply)
    return (-(partial_term[0] + outer_term[0]), -(partial_term[1] + outer_term[1]))


def kernel_piece(skew_grad, angles, tap_count):
    sym_real = skew_grad[0] - jnp.swapaxes(skew_grad[0], 1, 2)
    sym_imag = skew_grad[1] + jnp.swapaxes(skew_grad[1], 1, 2)
    piece_sum = jnp.einsum(
        "ft,foi->toi", jnp.cos(angles), sym_real, precision=HIGHEST
    ) - jnp.einsum("ft,foi->toi", jnp.sin(angles), sym_imag, precision=HIGHEST)
    return piece_sum.reshape(tap_count, tap_count, sym_real.shape[1], sym_real.shape[2])


def per_device(images, cotangent, kernel):
    side_cells = images.shape[1]
    channels = images.shape[3]
    half_cells = side_cells // 2 + 1
    tap_count = kernel.shape[0]
    across_angle, square_angle = angle_tables(side_cells, half_cells)
    image_spectrum = forward_spectrum(images, across_angle, square_angle)
    tangent_spectrum = forward_spectrum(cotangent, across_angle, square_angle)
    image_owned, tangent_owned = (
        lax.all_to_all(image_spectrum, "freq", split_axis=1, concat_axis=0, tiled=True),
        lax.all_to_all(tangent_spectrum, "freq", split_axis=1, concat_axis=0, tiled=True),
    )
    group_count = image_owned.shape[0]
    row_count = image_owned.shape[1]
    owned_count = row_count * half_cells
    row_numbers = lax.axis_index("freq") * row_count + jnp.arange(row_count, dtype=jnp.int32)
    angles = tap_angles(row_numbers, side_cells, half_cells, tap_count)
    skew_part = skew_matrix(kernel, angles)
    deviation = cayley_deviation(skew_part)
    operator = embedded(deviation)
    image_rows = image_owned.reshape(group_count, owned_count, 2 * channels)
    tangent_rows = tangent_owned.reshape(group_count, owned_count, 2 * channels)
    answer = jnp.einsum("nfj,fkj->nfk", image_rows, operator, preferred_element_type=jnp.float32)
    answer = (answer + image_rows.astype(jnp.float32)).astype(jnp.bfloat16)
    answer = answer.reshape(group_count, row_count, half_cells, 2 * channels)
    returned = lax.all_to_all(answer, "freq", split_axis=0, concat_axis=1, tiled=True)
    outputs = inverse_spectrum(returned, across_angle, square_angle)
    outer_sum = jnp.einsum(
        "nfk,nfj->fkj", tangent_rows, image_rows, preferred_element_type=jnp.float32
    )
    total_images = group_count * lax.axis_size("sample")
    factor = jnp.tile(grad_factor(side_cells, half_cells, total_images), row_count)
    grad_real = (outer_sum[:, :channels, :channels] + outer_sum[:, channels:, channels:]) * factor[
        :, None, None
    ]
    grad_imag = (outer_sum[:, channels:, :channels] - outer_sum[:, :channels, channels:]) * factor[
        :, None, None
    ]
    spec_grad = lax.psum((grad_real, grad_imag), "sample")
    piece_sum = kernel_piece(skew_gradient(spec_grad, deviation), angles, tap_count)
    kernel_grad = lax.psum(piece_sum, "freq")
    return (outputs, kernel_grad)


def solution(mesh):
    placed = (P(("sample", "freq"), None, None, None), P(("sample", "freq"), None, None, None), P())
    return jax.shard_map(
        per_device,
        mesh=mesh,
        in_specs=placed,
        out_specs=(P(("sample", "freq"), None, None, None), P()),
        check_vma=False,
    )
```

profile of v0, /device:TPU:0, one launch (start us, length us, event | category | flops | bytes accessed | tf_op | source)
XLA Modules:
  0.0 603.0 jit_solution(18246131588368750320)
XLA Ops:
  7.4 1.3 copy-done
  8.8 2.4 convolution_bitcast_fusion
  11.2 0.8 copy.413
  12.0 4.1 fusion.9
  16.1 3.1 copy.492
  19.2 6.0 reshape.221
  25.3 11.7 %all-to-all-start.2 = ((bf16[8,32,17,256]{3,0,2,1:T(8,128)(2,1)}), bf16[8,32,17,256]{3,0,2,1:T(8,128)(2,1)}, u32[]{:S(2)}, u32[]{:S(2)}) async-start(bf16[8,32,17,256]{3,0,2,1:T(8,128)(2,1)} %reshape.221), calls=%async_computation.2 | async-start | bytes 4456448 | tf_op jit(solution)/shard_map/all_to_all | solution.py:165
  37.0 2.2 convolution_bitcast_fusion.2
  39.3 2.2 convolution_bitcast_fusion.3
  41.7 1.4 copy.366
  43.1 3.1 fusion.141
  46.2 2.6 copy.372
  48.8 1.4 copy.371
  50.2 2.8 add.245
  52.9 2.6 copy.377
  55.6 1.4 copy.361
  57.0 2.2 negate_convert_fusion.1
  59.3 1.4 fusion.144
  61.0 1.3 copy-done.29
  62.3 2.3 convolution_bitcast_fusion.1
  64.6 0.8 copy.401
  65.4 4.3 fusion.7
  69.8 1.3 fusion.68
  71.1 1.3 fusion.147
  72.4 3.2 copy.486
  75.6 6.0 reshape.220
  81.6 1.8 fusion.45
  84.5 1.4 fusion.143
  85.9 1.4 fusion.146
  88.1 1.9 fusion.140
  90.0 0.8 copy-done.6
  90.8 1.4 fusion.148
  92.2 10.2 %all-to-all-start = ((bf16[8,32,17,256]{3,0,2,1:T(8,128)(2,1)}), bf16[8,32,17,256]{3,0,2,1:T(8,128)(2,1)}, u32[]{:S(2)}, u32[]{:S(2)}) async-start(bf16[8,32,17,256]{3,0,2,1:T(8,128)(2,1)} %reshape.220), calls=%async_computation | async-start | bytes 4456448 | tf_op jit(solution)/shard_map/all_to_all | solution.py:164
  102.5 2.2 fusion.69
  105.1 1.1 copy-done.7
  108.5 1.9 fusion.139
  110.5 24.3 %all-to-all-done = bf16[8,32,17,256]{3,0,2,1:T(8,128)(2,1)} async-done(((bf16[8,32,17,256]{3,0,2,1:T(8,128)(2,1)}), bf16[8,32,17,256]{3,0,2,1:T(8,128)(2,1)}, u32[]{:S(2)}, u32[]{:S(2)}) %all-to-all-start) | async-done | bytes 2228256 | tf_op jit(solution)/shard_map/all_to_all | solution.py:164
  134.7 3.1 fusion.18
  137.9 1.7 fusion.60
  139.6 1.0 copy-done.30
  140.8 3.8 fusion.8
  144.7 3.0 copy.407
  147.7 4.8 all-to-all-start.1
  152.9 4.0 fusion.61
  156.9 58.5 %all-to-all-done.1 = bf16[256,1,17,256]{3,2,1,0:T(8,128)(2,1)} async-done(((bf16[256,1,17,256]{3,2,1,0:T(8,128)(2,1)}), bf16[256,1,17,256]{3,2,1,0:T(8,128)(2,1)}, u32[]{:S(2)}, u32[]{:S(2)}) %all-to-all-start.1) | async-done | bytes 2228256 | tf_op jit(solution)/shard_map/all_to_all | solution.py:180
  215.4 4.6 copy.539
  220.0 5.7 reshape.199
  225.8 3.7 fusion.152
  229.5 2.4 fusion.150
  232.0 2.5 fusion.54
  234.4 2.0 fusion.153
  236.4 2.4 fusion.55
  238.9 2.0 fusion.151
  240.9 2.2 fusion.51
  243.1 3.1 fusion.53
  246.2 2.7 copy.425
  248.9 2.4 bitcast_subtract_fusion
  251.7 1.7 fusion.40
  253.5 1.7 fusion.56
  255.2 1.0 copy.431
  256.2 3.6 fusion.25
  260.5 7.5 %convert_bitcast_fusion = bf16[8,32,32,128]{3,2,1,0:T(8,128)(2,1)} fusion(f32[8,32,34,128]{3,1,2,0:T(8,128)S(1)} %bitcast.209, f32[17,32]{0,1:T(8,128)S(1)} %get-tuple-element.23, f32[17,32]{0,1:T(8,128)S(1)} %get-tuple-element.22), kind=kOutput, calls=%fused_computation.32 | convolution fusion | flops 428868672 | bytes 6557952 | tf_op jit(solution)/shard_map/nhkc,kw->nhwc/dot_general | solution.py:59
  268.0 326.0 %all-reduce.4.cloned.1.call-done = f32[3,3,128,128]{3,2,1,0:T(8,128)} async-done(((f32[3,3,128,128]{3,2,1,0:T(8,128)}), f32[3,3,128,128]{3,2,1,0:T(8,128)}) %all-reduce.4.cloned.1.call-update) | async-done | bytes 589840 | tf_op jit(solution)/shard_map/psum | solution.py:195
  594.0 1.9 copy.543
  (90 shorter events, 7.4 us)
Async XLA Ops:
  7.2 1.6 copy-start
  25.3 11.8 %copy-start.28 = (f32[3,3,128,128]{3,2,1,0:T(8,128)S(1)}, f32[3,3,128,128]{3,2,1,0:T(8,128)}, u32[]{:S(2)}) copy-start(f32[3,3,128,128]{3,2,1,0:T(8,128)} %param.5) | copy-start | bytes 1769476
  25.3 66.9 %all-to-all-start.2 = ((bf16[8,32,17,256]{3,0,2,1:T(8,128)(2,1)}), bf16[8,32,17,256]{3,0,2,1:T(8,128)(2,1)}, u32[]{:S(2)}, u32[]{:S(2)}) async-start(bf16[8,32,17,256]{3,0,2,1:T(8,128)(2,1)} %reshape.221), calls=%async_computation.2 | async-start | bytes 4456448 | tf_op jit(solution)/shard_map/all_to_all | solution.py:165
  39.2 2.2 copy-start.3
  41.5 14.1 %copy-start.2 = (f32[17,128,128]{2,0,1:T(8,128)}, f32[17,128,128]{2,0,1:T(8,128)S(1)}, u32[]{:S(2)}) copy-start(f32[17,128,128]{2,0,1:T(8,128)S(1)} %convolution_bitcast_fusion.3) | copy-start | bytes 3342340
  59.1 1.5 copy-start.10
  59.1 10.6 %copy-start.4 = (bf16[17,128,128]{2,1,0:T(8,128)(2,1)}, bf16[17,128,128]{2,1,0:T(8,128)(2,1)S(1)}, u32[]{:S(2)}) copy-start(bf16[17,128,128]{2,1,0:T(8,128)(2,1)S(1)} %get-tuple-element.15) | copy-start | bytes 1671172
  59.3 11.8 %copy-start.12 = (bf16[17,128,128]{2,1,0:T(8,128)(2,1)}, bf16[17,128,128]{2,1,0:T(8,128)(2,1)S(1)}, u32[]{:S(2)}) copy-start(bf16[17,128,128]{2,1,0:T(8,128)(2,1)S(1)} %negate_convert_fusion) | copy-start | bytes 1671172
  60.7 1.6 copy-start.29
  65.4 4.4 copy-start.15
  71.1 1.3 copy-start.23
  81.6 1.8 copy-start.13
  83.4 1.1 copy-start.24
  84.4 1.4 copy-start.11
  84.5 2.8 copy-start.25
  85.9 1.4 copy-start.8
  85.9 1.9 copy-start.14
  85.9 2.2 copy-start.16
  90.0 0.8 copy-start.6
  92.2 10.2 %copy-start.5 = (bf16[17,128,128]{2,1,0:T(8,128)(2,1)S(1)}, bf16[17,128,128]{2,1,0:T(8,128)(2,1)}, u32[]{:S(2)}) copy-start(bf16[17,128,128]{2,1,0:T(8,128)(2,1)} %copy-done.4) | copy-start | bytes 1671172
  92.2 42.5 %all-to-all-start = ((bf16[8,32,17,256]{3,0,2,1:T(8,128)(2,1)}), bf16[8,32,17,256]{3,0,2,1:T(8,128)(2,1)}, u32[]{:S(2)}, u32[]{:S(2)}) async-start(bf16[8,32,17,256]{3,0,2,1:T(8,128)(2,1)} %reshape.220), calls=%async_computation | async-start | bytes 4456448 | tf_op jit(solution)/shard_map/all_to_all | solution.py:164
  102.4 123.4 %all-reduce.6.cloned.1.call-start = ((), (), s32[]{:S(2)}) async-start(), calls=%async_computation.4 | async-start | bytes 4456448 | tf_op jit(solution)/shard_map/psum | solution.py:193
  102.5 2.3 copy-start.9
  102.5 2.6 copy-start.27
  104.7 3.0 copy-start.17
  104.7 1.5 copy-start.7
  104.7 1.8 copy-start.20
  107.3 1.2 copy-start.19
  139.6 1.1 copy-start.30
  139.6 1.2 copy-start.31
  147.7 67.7 %all-to-all-start.1 = ((bf16[256,1,17,256]{3,2,1,0:T(8,128)(2,1)}), bf16[256,1,17,256]{3,2,1,0:T(8,128)(2,1)}, u32[]{:S(2)}, u32[]{:S(2)}) async-start(bf16[256,1,17,256]{3,2,1,0:T(8,128)(2,1)} %copy.407), calls=%async_computation.1 | async-start | bytes 6291456 | tf_op jit(solution)/shard_map/all_to_all | solution.py:180
  152.5 441.5 %all-reduce.4.cloned.1.call-start = ((), (), s32[]{:S(2)}) async-start(), calls=%async_computation.3 | async-start | bytes 1179648 | tf_op jit(solution)/shard_map/psum | solution.py:195
  225.7 3.8 copy-start.18
  229.5 2.4 copy-start.26
  246.2 2.7 copy-start.21
  251.7 1.7 copy-start.22
  260.5 335.5 %copy-start.1 = (bf16[8,32,32,128]{3,2,1,0:T(8,128)(2,1)S(1)}, bf16[8,32,32,128]{3,2,1,0:T(8,128)(2,1)}, u32[]{:S(2)}) copy-start(bf16[8,32,32,128]{3,2,1,0:T(8,128)(2,1)} %param.4) | copy-start | bytes 6291460
Sparse Core Ops, SparseCore 0:
  139.8 77.6 all-reduce.5
  256.3 337.6 all-reduce.3
where the time goes:
time: 611 us; the launch traced here: 603 us
  waiting for transfers between devices  409 us (67%)
  matrix products  77.5 us (13%)
  local copies, waits for them, and re-layouts  58 us (9%)
  starting transfers between devices  26.7 us (4%)
  other arithmetic  17.1 us (3%)
  between operations  14.8 us (2%)
    psum x1, waiting for transfers between devices, per_device(): kernel_grad = lax.psum(piece_sum, 'freq')  326 us
    all_to_all x1, waiting for transfers between devices, per_device(): lax.all_to_all(answer, 'freq', split_axis=0, concat_axis=1, tiled=True)  58.5 us
    all_to_all x1, waiting for transfers between devices, per_device(): lax.all_to_all(image_spectrum, 'freq', split_axis=1, concat_axis=0, tiled...  24.3 us
    dot_general x8, matrix products, full_multiply(): return jnp.einsum('fij,fjk->fik', former, latter, precision=HIGHEST)  20.3 us
    convert_element_type x4, local copies, waits for them, and re-layouts, forward_spectrum(): spectrum.reshape(number, side_cells, half_cells, 2 * channels)  18.3 us
    dot_general x16, matrix products, low_multiply(): jnp.einsum('fij,fjk->fik', former.astype(jnp.bfloat16), latter.astype(jnp...  18.1 us
  transfers between devices with their start and end apart: 5, of which 3 were waited for; matrix products, arithmetic and copies ran while one was open for 15% of the time, Pallas kernels for 0%

commit v1 on v0

v1 whole, which is shorter than its diff:
```python
import functools
import math

import jax
import jax.numpy as jnp
import numpy as np
from jax import lax
from jax.experimental import pallas as pl
from jax.experimental.pallas import tpu as pltpu
from jax.sharding import PartitionSpec as P

NS_STEPS = 2


def transform_tables(side, images):
    half = side // 2
    freq = np.arange(half)
    cell = np.arange(side)
    angle = 2.0 * math.pi / side * ((freq[:, None] * cell[None, :]) % side)
    real_rows = np.cos(angle)
    imag_rows = -np.sin(angle)
    imag_rows[0] = np.where(cell % 2 == 0, 1.0, -1.0)
    forward = np.stack([real_rows, imag_rows])
    weight = np.full((2, half, 1), 2.0 / side)
    weight[:, 0] = 1.0 / side
    same = np.eye(images)
    analysis = np.einsum("asw,nm->asnmw", forward, same).reshape(side * images, images * side)
    synthesis = np.einsum("asw,nm->nwasm", forward * weight, same).reshape(images * side, side * images)
    return analysis, synthesis


def slot_tables(side, total_images):
    half = side // 2
    angle = 2.0 * math.pi / side * np.arange(half)
    cos_a, cos_b, sine = np.cos(angle), np.cos(angle), np.sin(angle)
    cos_b[0] = -1.0
    sine[0] = 0.0
    scale = np.full(half, -2.0 * 2.0 / (total_images * side))
    scale[0] *= 0.5
    return np.stack([cos_a, cos_b, sine, scale]).astype(np.float32)


def local_kernel(
    images, channels, side, group, slot_table, pictures_hbm, cotangent_hbm, taps_hbm, analysis_hbm, synthesis_hbm,
    outputs_hbm, pieces_ref,
    pictures, cotangent, taps, analysis, synthesis, mixes, weights, base, state, other, partner, answer, total,
    result, in_sem, out_sem,
):
    half = side // 2
    pair = 2 * images
    rows = side * pair
    wide = 2 * channels

    loads = [
        pltpu.make_async_copy(taps_hbm, taps, in_sem.at[0]),
        pltpu.make_async_copy(analysis_hbm, analysis, in_sem.at[1]),
        pltpu.make_async_copy(pictures_hbm, pictures, in_sem.at[2]),
        pltpu.make_async_copy(cotangent_hbm, cotangent, in_sem.at[3]),
        pltpu.make_async_copy(synthesis_hbm, synthesis, in_sem.at[4]),
    ]
    for load in loads:
        load.start()
    loads[0].wait()
    for row in range(3):
        across = [taps[row, col].T - taps[2 - row, 2 - col] for col in range(3)]
        mixes[row, 0] = across[1]
        mixes[row, 1] = across[2] + across[0]
        mixes[row, 2] = across[0] - across[2]
    total[...] = jnp.zeros_like(total)
    for load in loads[1:4]:
        load.wait()

    def analyse(h, carry):
        both = jnp.concatenate(
            [pictures[:, h].reshape(images * side, channels), cotangent[:, h].reshape(images * side, channels)], axis=1
        )
        spectrum = jnp.dot(analysis[...], both, preferred_element_type=jnp.float32)
        spectrum = spectrum.reshape(2, half, images, wide)
        spectrum = jnp.concatenate([spectrum[..., :channels], spectrum[..., channels:]], axis=2).astype(jnp.bfloat16)
        where = pl.ds(pl.multiple_of((h + 1) * pair, pair), pair)
        base[:, where, :channels] = spectrum[0]
        base[:, where, channels:] = spectrum[1]
        return carry

    lax.fori_loop(0, side, analyse, 0, unroll=4)
    base[:, :pair] = base[:, rows : rows + pair]
    base[:, rows + pair :] = base[:, pair : 2 * pair]

    def apply(source, weight):
        stacked = jnp.concatenate([source[2 * pair :], source[pair : rows + pair], source[:rows]], axis=1)
        return jnp.dot(stacked, weight, preferred_element_type=jnp.float32)

    def slot_group(index, carry):
        slots = [index * group + lane for lane in range(group)]
        for lane, slot in enumerate(slots):
            cos_a, cos_b, sine = slot_table[0, slot], slot_table[1, slot], slot_table[2, slot]
            for row in range(3):
                turned = (sine * mixes[row, 2]).astype(jnp.bfloat16)
                lo, hi = row * wide, row * wide + channels
                weights[lane, lo:hi, :channels] = (mixes[row, 0] + cos_a * mixes[row, 1]).astype(jnp.bfloat16)
                weights[lane, hi : hi + channels, channels:] = (mixes[row, 0] + cos_b * mixes[row, 1]).astype(jnp.bfloat16)
                weights[lane, lo:hi, channels:] = turned
                weights[lane, hi : hi + channels, :channels] = -turned
        powers = 2 ** (NS_STEPS + 1) - 1
        for step in range(powers):
            for lane, slot in enumerate(slots):
                source = base.at[slot] if step == 0 else (state if step % 2 else other).at[lane]
                target = (other if step % 2 else state).at[lane]
                product = apply(source, weights[lane]).reshape(side, 2, images, wide)
                start = base[slot, pair : rows + pair].astype(jnp.float32).reshape(side, 2, images, wide)
                forward = start[:, 0] - product[:, 0]
                backward = start[:, 1] + product[:, 1]
                joined = jnp.stack([forward, backward], axis=1).reshape(rows, wide).astype(jnp.bfloat16)
                target[pair : rows + pair] = joined
                if step < powers - 1:
                    target[:pair] = joined[rows - pair :]
                    target[rows + pair :] = joined[:pair]
                else:
                    answer[slot] = (2.0 * forward - start[:, 0]).reshape(side * images, wide)
                    crossed = jnp.stack([-backward, forward], axis=1).reshape(rows, wide).astype(jnp.bfloat16)
                    partner[lane, pair:] = crossed
                    partner[lane, :pair] = crossed[rows - pair :]
        last = state if powers % 2 else other
        for lane, slot in enumerate(slots):
            cos_a, cos_b, sine, scale = (slot_table[k, slot] for k in range(4))
            left = last[lane, pair : rows + pair]
            for row, right in enumerate((partner[lane, pair:], partner[lane, :rows])):
                outer = lax.dot_general(left, right, (((0,), (0,)), ((), ())), preferred_element_type=jnp.float32)
                outer = outer * scale
                first, second = outer[:channels, :channels], outer[channels:, channels:]
                total[row, 0] += first + second
                total[row, 1] += cos_a * first + cos_b * second
                total[row, 2] += sine * (outer[channels:, :channels] - outer[:channels, channels:])
        return carry

    lax.fori_loop(0, half // group, slot_group, 0)

    pieces_ref[0] = total[0, 0]
    pieces_ref[1] = total[0, 1] - total[0, 2]
    pieces_ref[2] = total[1, 0]
    pieces_ref[3] = total[1, 1] - total[1, 2]
    pieces_ref[4] = total[1, 1] + total[1, 2]
    loads[4].wait()

    def synthesise(index, carry):
        columns = []
        for part in range(2):
            where = pl.ds(pl.multiple_of((2 * index + part) * images, images), images)
            tiles = [answer[:, where, k * channels : (k + 1) * channels].reshape(half * images, channels) for k in range(2)]
            columns.append(jnp.concatenate(tiles, axis=0).astype(jnp.bfloat16))
        maps = jnp.dot(synthesis[...], jnp.concatenate(columns, axis=1), preferred_element_type=jnp.float32)
        maps = maps.astype(jnp.bfloat16)
        for part in range(2):
            result[:, 2 * index + part] = maps[:, part * channels : (part + 1) * channels].reshape(images, side, channels)
        return carry

    lax.fori_loop(0, side // 2, synthesise, 0, unroll=4)
    store = pltpu.make_async_copy(result, outputs_hbm, out_sem)
    store.start()
    store.wait()


def local_work(pictures, cotangent, kernel, total_images, group=2):
    images, side, _, channels = pictures.shape
    half = side // 2
    pair = 2 * images
    rows = side * pair
    wide = 2 * channels
    analysis, synthesis = transform_tables(side, images)
    analysis = jnp.asarray(analysis, jnp.bfloat16)
    synthesis = jnp.asarray(synthesis, jnp.bfloat16)
    table = jnp.asarray(slot_tables(side, total_images))
    anywhere = pl.BlockSpec(memory_space=pl.ANY)
    return pl.pallas_call(
        functools.partial(local_kernel, images, channels, side, group),
        out_shape=(
            jax.ShapeDtypeStruct(pictures.shape, jnp.bfloat16),
            jax.ShapeDtypeStruct((5, channels, channels), jnp.float32),
        ),
        in_specs=[pl.BlockSpec(memory_space=pltpu.SMEM)] + [anywhere] * 5,
        out_specs=(anywhere, pl.BlockSpec(memory_space=pltpu.VMEM)),
        scratch_shapes=[
            pltpu.VMEM(pictures.shape, jnp.bfloat16),
            pltpu.VMEM(pictures.shape, jnp.bfloat16),
            pltpu.VMEM(kernel.shape, jnp.float32),
            pltpu.VMEM((wide, wide), jnp.bfloat16),
            pltpu.VMEM((wide, wide), jnp.bfloat16),
            pltpu.VMEM((3, 3, channels, channels), jnp.float32),
            pltpu.VMEM((group, 3 * wide, wide), jnp.bfloat16),
            pltpu.VMEM((half, rows + 2 * pair, wide), jnp.bfloat16),
            pltpu.VMEM((group, rows + 2 * pair, wide), jnp.bfloat16),
            pltpu.VMEM((group, rows + 2 * pair, wide), jnp.bfloat16),
            pltpu.VMEM((group, rows + pair, wide), jnp.bfloat16),
            pltpu.VMEM((half, side * images, wide), jnp.float32),
            pltpu.VMEM((2, 3, channels, channels), jnp.float32),
            pltpu.VMEM(pictures.shape, jnp.bfloat16),
            pltpu.SemaphoreType.DMA((5,)),
            pltpu.SemaphoreType.DMA,
        ],
        compiler_params=pltpu.CompilerParams(vmem_limit_bytes=48 * 1024 * 1024),
        name="local_work",
    )(table, pictures, cotangent, kernel, analysis, synthesis)


def per_device(images, cotangent, kernel):
    total = images.shape[0] * lax.axis_size("sample") * lax.axis_size("freq")
    outputs, pieces = local_work(images, cotangent, kernel, total)
    pieces = lax.psum(pieces, ("sample", "freq"))
    flip = -jnp.swapaxes(pieces, 1, 2)
    kernel_grad = jnp.stack(
        [flip[3], flip[2], flip[4], flip[1], pieces[0], pieces[1], pieces[4], pieces[2], pieces[3]]
    )
    return outputs, kernel_grad.reshape(kernel.shape)


def solution(mesh):
    placed = P(("sample", "freq"), None, None, None)
    return jax.shard_map(
        per_device,
        mesh=mesh,
        in_specs=(placed, placed, P()),
        out_specs=(placed, P()),
        check_vma=False,
    )
```

time: 611 us -> 207 us (0.34)
  the two profiles are of different devices: /device:TPU:0 before, /device:TPU:1 now
where the time goes in v1:
time: 207 us
  waiting for transfers between devices  147 us (71%)
  Pallas kernels  35.8 us (17%)
  between operations  14.1 us (7%)
  local copies, waits for them, and re-layouts  9.71 us (5%)
    psum x1, waiting for transfers between devices, per_device(): pieces = lax.psum(pieces, ('sample', 'freq'))  147 us
    pallas_call x1, Pallas kernels, local_work(): pl.pallas_call(functools.partial(local_kernel, images, channels, side, gr...  35.8 us
    unnamed x22, local copies, waits for them, and re-layouts  8.49 us
  transfers between devices with their start and end apart: 1, of which 1 were waited for; matrix products, arithmetic and copies ran while one was open for 0% of the time, Pallas kernels for 0%

profile of v1, /device:TPU:1, one launch (start us, length us, event | category | flops | bytes accessed | tf_op | source)
XLA Modules:
  0.0 206.5 jit_solution(8180887791699891299)
XLA Ops:
  7.2 0.0 all-reduce.2.cloned.1.call-start
  7.2 0.0 copy-start
  7.2 1.6 copy-done
  8.8 0.0 copy-start.1
  8.8 1.6 copy-done.1
  10.4 0.0 copy-start.2
  10.4 1.1 copy-done.2
  11.5 0.0 copy-start.3
  11.5 0.9 copy-done.3
  12.4 0.0 copy-start.4
  12.4 0.9 copy-done.4
  13.3 0.0 copy-start.5
  13.3 0.7 copy-done.5
  13.9 35.8 %local_work.1 = (bf16[8,32,32,128]{3,2,1,0:T(8,128)(2,1)}, f32[5,128,128]{2,1,0:T(8,128)}) custom-call(f32[4,16]{1,0:T(4,128)S(1)} %copy-done.5, bf16[8,32,32,128]{3,2,1,0:T(8,128)(2,1)S(1)} %copy-done, bf16[8,32,32,128]{3,2,1,0:T(8,128)(2,1)S(1)} %copy-done.1, f32[3,3,128,128]{3,2,1,0:T(8,128)S(1)} %copy-done.2, bf16[256,256]{1,0:T(8,128)(2,1)S(1)} %copy-done.4, ...), custom_call_target="tpu_custom_call" | custom-call | tf_op jit(solution)/shard_map/local_work/pallas_call | solution.py:174
  49.8 0.0 all-reduce.2.cloned.1.call-update
  49.8 146.8 %all-reduce.2.cloned.1.call-done = f32[5,128,128]{2,1,0:T(8,128)} async-done(((f32[5,128,128]{2,1,0:T(8,128)}), f32[5,128,128]{2,1,0:T(8,128)}) %all-reduce.2.cloned.1.call-update) | async-done | bytes 327696 | tf_op jit(solution)/shard_map/psum | solution.py:208
  196.6 0.0 copy-start.6
  196.6 1.2 copy.8
  197.9 0.9 slice_dynamic-update-slice_fusion.1
  198.8 0.0 copy-done.6
  198.9 0.0 copy-start.7
  198.9 0.8 copy-done.7
  (7 shorter events, 0.1 us)
Async XLA Ops:
  7.2 189.4 %all-reduce.2.cloned.1.call-start = ((), (), s32[]{:S(2)}) async-start(), calls=%async_computation | async-start | bytes 655360 | tf_op jit(solution)/shard_map/psum | solution.py:208
  7.2 1.6 copy-start
  8.8 1.6 copy-start.1
  10.4 1.1 copy-start.2
  11.5 0.9 copy-start.3
  12.4 0.9 copy-start.4
  13.3 0.7 copy-start.5
  196.6 2.2 %copy-start.6 = (f32[5,128,128]{2,1,0:T(8,128)S(1)}, f32[5,128,128]{2,1,0:T(8,128)}, u32[]{:S(2)}) copy-start(f32[5,128,128]{2,1,0:T(8,128)} %all-reduce.2.cloned.1.call-done) | copy-start | bytes 983044
  198.9 0.8 copy-start.7
Sparse Core Ops, SparseCore 0:
  49.9 146.6 all-reduce.1

commit v2 on v1

--- a/solution.py
+++ b/solution.py
@@ -10,6 +10,7 @@
 from jax.sharding import PartitionSpec as P
 
 NS_STEPS = 2
+GAIN = 1.6245
 
 
 def transform_tables(side, images):
@@ -26,7 +27,7 @@
     same = np.eye(images)
     analysis = np.einsum("asw,nm->asnmw", forward, same).reshape(side * images, images * side)
     synthesis = np.einsum("asw,nm->nwasm", forward * weight, same).reshape(images * side, side * images)
-    return analysis, synthesis
+    return GAIN * analysis, GAIN * synthesis
 
 
 def slot_tables(side, total_images):
@@ -35,21 +36,45 @@
     cos_a, cos_b, sine = np.cos(angle), np.cos(angle), np.sin(angle)
     cos_b[0] = -1.0
     sine[0] = 0.0
-    scale = np.full(half, -2.0 * 2.0 / (total_images * side))
+    scale = np.full(half, -2.0 * 2.0 / (total_images * side * GAIN**2))
     scale[0] *= 0.5
     return np.stack([cos_a, cos_b, sine, scale]).astype(np.float32)
 
 
-def local_kernel(
+def layer_kernel(
     images, channels, side, group, slot_table, pictures_hbm, cotangent_hbm, taps_hbm, analysis_hbm, synthesis_hbm,
-    outputs_hbm, pieces_ref,
+    outputs_hbm, kernel_grad,
     pictures, cotangent, taps, analysis, synthesis, mixes, weights, base, state, other, partner, answer, total,
-    result, in_sem, out_sem,
+    result, chunks, from_partner, mine, received, gathered, in_sem, out_sem, core_sem, chip_send, chip_recv,
 ):
     half = side // 2
     pair = 2 * images
     rows = side * pair
     wide = 2 * channels
+    sample, freq = lax.axis_index("sample"), lax.axis_index("freq")
+    ring = lax.axis_size("freq")
+    chips = lax.axis_size("sample") * ring // 2
+    core = sample % 2
+    chip = sample // 2 * ring + freq
+
+    def place_of(to_chip, to_core):
+        return (to_chip // ring * 2 + to_core, to_chip % ring)
+
+    def remote(source, target, send, recv, to_chip, to_core):
+        return pltpu.make_async_remote_copy(
+            source, target, send, recv, device_id=place_of(to_chip, to_core), device_id_type=pl.DeviceIdType.MESH
+        )
+
+    barrier = pltpu.get_barrier_semaphore()
+
+    def greet(ahead, carry):
+        pl.semaphore_signal(
+            barrier, inc=1, device_id=place_of((chip + ahead) % chips, core), device_id_type=pl.DeviceIdType.MESH
+        )
+        return carry
+
+    lax.fori_loop(1, chips, greet, 0)
+    pl.semaphore_signal(barrier, inc=1, device_id=place_of(chip, 1 - core), device_id_type=pl.DeviceIdType.MESH)
 
     loads = [
         pltpu.make_async_copy(taps_hbm, taps, in_sem.at[0]),
@@ -116,7 +141,8 @@
                     target[:pair] = joined[rows - pair :]
                     target[rows + pair :] = joined[:pair]
                 else:
-                    answer[slot] = (2.0 * forward - start[:, 0]).reshape(side * images, wide)
+                    finished = (2.0 / GAIN**2) * forward - (1.0 / GAIN**2) * start[:, 0]
+                    answer[slot] = finished.reshape(side * images, wide)
                     crossed = jnp.stack([-backward, forward], axis=1).reshape(rows, wide).astype(jnp.bfloat16)
                     partner[lane, pair:] = crossed
                     partner[lane, :pair] = crossed[rows - pair :]
@@ -135,11 +161,17 @@
 
     lax.fori_loop(0, half // group, slot_group, 0)
 
-    pieces_ref[0] = total[0, 0]
-    pieces_ref[1] = total[0, 1] - total[0, 2]
-    pieces_ref[2] = total[1, 0]
-    pieces_ref[3] = total[1, 1] - total[1, 2]
-    pieces_ref[4] = total[1, 1] + total[1, 2]
+    def lay(place, piece):
+        chunks[:, :, place] = piece.reshape(2, chips, channels)
+
+    lay(0, total[0, 0])
+    lay(1, total[0, 1] - total[0, 2])
+    lay(2, total[1, 0])
+    lay(3, total[1, 1] - total[1, 2])
+    lay(4, total[1, 1] + total[1, 2])
+    pl.semaphore_wait(barrier, chips)
+    swap = remote(chunks.at[1 - core], from_partner, core_sem.at[0], core_sem.at[1], chip, 1 - core)
+    swap.start()
     loads[4].wait()
 
     def synthesise(index, carry):
@@ -154,13 +186,49 @@
             result[:, 2 * index + part] = maps[:, part * channels : (part + 1) * channels].reshape(images, side, channels)
         return carry
 
-    lax.fori_loop(0, side // 2, synthesise, 0, unroll=4)
+    third = side // 6
+    lax.fori_loop(0, third, synthesise, 0, unroll=True)
+    swap.wait()
+    mine[...] = chunks[core] + from_partner[...]
+
+    def scatter(ahead, carry):
+        there = (chip + ahead) % chips
+        remote(mine.at[there], received.at[ahead - 1], chip_send.at[0], chip_recv.at[0], there, core).start()
+        return carry
+
+    lax.fori_loop(1, chips, scatter, 0)
+    lax.fori_loop(third, 2 * third, synthesise, 0, unroll=True)
+    everything = pltpu.make_async_copy(received, received, chip_recv.at[0])
+    everything.wait()
+    pltpu.make_async_copy(received, received, chip_send.at[0]).wait()
+    gathered[core, chip] = mine[chip] + jnp.sum(received[...], axis=0)
+
+    def spread(ahead, carry):
+        there = (chip + ahead) % chips
+        piece = gathered.at[core, chip]
+        remote(piece, piece, chip_send.at[1], chip_recv.at[1], there, core).start()
+        return carry
+
+    lax.fori_loop(1, chips, spread, 0)
+    lax.fori_loop(2 * third, side // 2, synthesise, 0, unroll=True)
     store = pltpu.make_async_copy(result, outputs_hbm, out_sem)
     store.start()
+    pltpu.make_async_copy(received, received, chip_recv.at[1]).wait()
+    pltpu.make_async_copy(received, received, chip_send.at[1]).wait()
+    ours = gathered.at[core]
+    swap = remote(ours, ours, core_sem.at[2], core_sem.at[3], chip, 1 - core)
+    swap.start()
+    swap.wait()
+
+    sums = [gathered[:, :, place].reshape(channels, channels) for place in range(5)]
+    for place, (row, col) in enumerate(((1, 1), (1, 2), (2, 1), (2, 2), (2, 0))):
+        kernel_grad[row, col] = sums[place]
+        if place:
+            kernel_grad[2 - row, 2 - col] = -sums[place].T
     store.wait()
 
 
-def local_work(pictures, cotangent, kernel, total_images, group=2):
+def layer(pictures, cotangent, kernel, total_images, group=2):
     images, side, _, channels = pictures.shape
     half = side // 2
     pair = 2 * images
@@ -170,12 +238,13 @@
     analysis = jnp.asarray(analysis, jnp.bfloat16)
     synthesis = jnp.asarray(synthesis, jnp.bfloat16)
     table = jnp.asarray(slot_tables(side, total_images))
-    anywhere = pl.BlockSpec(memory_space=pl.ANY)
+    anywhere = pl.BlockSpec(memory_space=pltpu.HBM)
+    chips = lax.axis_size("sample") * lax.axis_size("freq") // 2
     return pl.pallas_call(
-        functools.partial(local_kernel, images, channels, side, group),
+        functools.partial(layer_kernel, images, channels, side, group),
         out_shape=(
             jax.ShapeDtypeStruct(pictures.shape, jnp.bfloat16),
-            jax.ShapeDtypeStruct((5, channels, channels), jnp.float32),
+            jax.ShapeDtypeStruct(kernel.shape, jnp.float32),
         ),
         in_specs=[pl.BlockSpec(memory_space=pltpu.SMEM)] + [anywhere] * 5,
         out_specs=(anywhere, pl.BlockSpec(memory_space=pltpu.VMEM)),
@@ -194,23 +263,25 @@
             pltpu.VMEM((half, side * images, wide), jnp.float32),
             pltpu.VMEM((2, 3, channels, channels), jnp.float32),
             pltpu.VMEM(pictures.shape, jnp.bfloat16),
+            pltpu.VMEM((2, chips, 5, channels), jnp.float32),
+            pltpu.VMEM((chips, 5, channels), jnp.float32),
+            pltpu.VMEM((chips, 5, channels), jnp.float32),
+            pltpu.VMEM((chips - 1, 5, channels), jnp.float32),
+            pltpu.VMEM((2, chips, 5, channels), jnp.float32),
             pltpu.SemaphoreType.DMA((5,)),
             pltpu.SemaphoreType.DMA,
+            pltpu.SemaphoreType.DMA((4,)),
+            pltpu.SemaphoreType.DMA((2,)),
+            pltpu.SemaphoreType.DMA((2,)),
         ],
-        compiler_params=pltpu.CompilerParams(vmem_limit_bytes=48 * 1024 * 1024),
-        name="local_work",
+        compiler_params=pltpu.CompilerParams(vmem_limit_bytes=63 * 1024 * 1024, collective_id=0, has_side_effects=True),
+        name="layer",
     )(table, pictures, cotangent, kernel, analysis, synthesis)
 
 
 def per_device(images, cotangent, kernel):
     total = images.shape[0] * lax.axis_size("sample") * lax.axis_size("freq")
-    outputs, pieces = local_work(images, cotangent, kernel, total)
-    pieces = lax.psum(pieces, ("sample", "freq"))
-    flip = -jnp.swapaxes(pieces, 1, 2)
-    kernel_grad = jnp.stack(
-        [flip[3], flip[2], flip[4], flip[1], pieces[0], pieces[1], pieces[4], pieces[2], pieces[3]]
-    )
-    return outputs, kernel_grad.reshape(kernel.shape)
+    return layer(images, cotangent, kernel, total)
 
 
 def solution(mesh):

time: 207 us -> 62.9 us (0.30)
  waiting for transfers between devices: 147 us -> 0 us
  Pallas kernels: 35.8 us -> 57.9 us
  between operations: 14.1 us -> 0.65 us
  local copies, waits for them, and re-layouts: 9.71 us -> 4.15 us
    psum x1 -> x0, waiting for transfers between devices: 147 us -> none  [per_device(): pieces = lax.psum(pieces, ('sample', 'freq'))]
    pallas_call x1, Pallas kernels: 35.8 us -> 57.9 us  [layer(): pl.pallas_call(functools.partial(layer_kernel, images, channels, side, gr...]
    unnamed x22 -> x4, local copies, waits for them, and re-layouts: 8.49 us -> 4.15 us
  transfers between devices with their start and end apart: 1 -> 0, of which waited for: 1 -> 0; matrix products, arithmetic and copies ran while one was open for 0% -> 0% of each run, Pallas kernels for 0% -> 0%
where the time goes in v2:
time: 62.9 us; the launch traced here: 62.7 us
  Pallas kernels  57.9 us (92%)
  local copies, waits for them, and re-layouts  4.15 us (7%)
  between operations  0.65 us (1%)
    pallas_call x1, Pallas kernels, layer(): pl.pallas_call(functools.partial(layer_kernel, images, channels, side, gr...  57.9 us
    unnamed x4, local copies, waits for them, and re-layouts  4.15 us

profile of v2, /device:TPU:1, one launch (start us, length us, event | category | flops | bytes accessed | tf_op | source)
XLA Modules:
  0.0 62.7 jit_solution(213489984613412631)
XLA Ops:
  0.6 57.9 %layer.1 = (bf16[8,32,32,128]{3,2,1,0:T(8,128)(2,1)}, f32[3,3,128,128]{3,2,1,0:T(8,128)}) custom-call(f32[4,16]{1,0:T(4,128)} %constant.8.clone.slot_table, bf16[8,32,32,128]{3,2,1,0:T(8,128)(2,1)} %pictures_hbm.1, bf16[8,32,32,128]{3,2,1,0:T(8,128)(2,1)} %cotangent_hbm.1, f32[3,3,128,128]{3,2,1,0:T(8,128)} %taps_hbm.1, ...), custom_call_target="tpu_custom_call" | custom-call | tf_op jit(solution)/shard_map/layer/pallas_call | solution.py:243
  58.5 0.0 copy-start
  58.6 3.3 %copy.10 = bf16[8,32,32,128]{3,2,1,0:T(8,128)(2,1)} copy(bf16[8,32,32,128]{3,2,1,0:T(8,128)(2,1)} %get-tuple-element.4) | data formatting | bytes 4194304
  61.9 0.0 copy-done
  61.9 0.8 %copy.11 = f32[3,3,128,128]{3,2,1,0:T(8,128)} copy(f32[3,3,128,128]{3,2,1,0:T(8,128)S(1)} %copy-done) | data formatting | bytes 1179648
Async XLA Ops:
  58.5 3.3 %copy-start = (f32[3,3,128,128]{3,2,1,0:T(8,128)S(1)}, f32[3,3,128,128]{3,2,1,0:T(8,128)}, u32[]{:S(2)}) copy-start(f32[3,3,128,128]{3,2,1,0:T(8,128)} %get-tuple-element.5) | copy-start | bytes 1769476

commit v3 on v2

--- a/solution.py
+++ b/solution.py
@@ -41,6 +41,11 @@
     return np.stack([cos_a, cos_b, sine, scale]).astype(np.float32)
 
 
+def hops(ahead, ring):
+    x = 2 * (ahead & 1) + ahead // ring
+    return sum((0, 1, 2, 1)[part] for part in (x, ahead // 8 % 4, ahead // 2 % 4))
+
+
 def layer_kernel(
     images, channels, side, group, slot_table, pictures_hbm, cotangent_hbm, taps_hbm, analysis_hbm, synthesis_hbm,
     outputs_hbm, kernel_grad,
@@ -66,15 +71,7 @@
         )
 
     barrier = pltpu.get_barrier_semaphore()
-
-    def greet(ahead, carry):
-        pl.semaphore_signal(
-            barrier, inc=1, device_id=place_of((chip + ahead) % chips, core), device_id_type=pl.DeviceIdType.MESH
-        )
-        return carry
-
-    lax.fori_loop(1, chips, greet, 0)
-    pl.semaphore_signal(barrier, inc=1, device_id=place_of(chip, 1 - core), device_id_type=pl.DeviceIdType.MESH)
+    far_first = sorted(range(1, chips), key=lambda ahead: -hops(ahead, ring))
 
     loads = [
         pltpu.make_async_copy(taps_hbm, taps, in_sem.at[0]),
@@ -92,6 +89,13 @@
         mixes[row, 1] = across[2] + across[0]
         mixes[row, 2] = across[0] - across[2]
     total[...] = jnp.zeros_like(total)
+
+    def greet(beside, carry):
+        there = place_of(chip ^ beside, jnp.where(beside == 0, 1 - core, core))
+        pl.semaphore_signal(barrier, inc=1, device_id=there, device_id_type=pl.DeviceIdType.MESH)
+        return carry
+
+    lax.fori_loop(0, chips, greet, 0, unroll=8)
     for load in loads[1:4]:
         load.wait()
 
@@ -115,51 +119,84 @@
         stacked = jnp.concatenate([source[2 * pair :], source[pair : rows + pair], source[:rows]], axis=1)
         return jnp.dot(stacked, weight, preferred_element_type=jnp.float32)
 
+    powers = 2 ** (NS_STEPS + 1) - 1
+    last = state if powers % 2 else other
+
+    def weigh(lane, slot):
+        cos_a, cos_b, sine = slot_table[0, slot], slot_table[1, slot], slot_table[2, slot]
+        for row in range(3):
+            turned = (sine * mixes[row, 2]).astype(jnp.bfloat16)
+            lo, hi = row * wide, row * wide + channels
+            weights[lane, lo:hi, :channels] = (mixes[row, 0] + cos_a * mixes[row, 1]).astype(jnp.bfloat16)
+            weights[lane, hi : hi + channels, channels:] = (mixes[row, 0] + cos_b * mixes[row, 1]).astype(jnp.bfloat16)
+            weights[lane, lo:hi, channels:] = turned
+            weights[lane, hi : hi + channels, :channels] = -turned
+
+    def power(lane, slot, step):
+        source = base.at[slot] if step == 0 else (state if step % 2 else other).at[lane]
+        target = (other if step % 2 else state).at[lane]
+        product = apply(source, weights[lane]).reshape(side, 2, images, wide)
+        start = base[slot, pair : rows + pair].astype(jnp.float32).reshape(side, 2, images, wide)
+        forward = start[:, 0] - product[:, 0]
+        backward = start[:, 1] + product[:, 1]
+        joined = jnp.stack([forward, backward], axis=1).reshape(rows, wide).astype(jnp.bfloat16)
+        target[pair : rows + pair] = joined
+        if step < powers - 1:
+            target[:pair] = joined[rows - pair :]
+            target[rows + pair :] = joined[:pair]
+        else:
+            finished = (2.0 / GAIN**2) * forward - (1.0 / GAIN**2) * start[:, 0]
+            answer[slot] = finished.reshape(side * images, wide)
+            crossed = jnp.stack([-backward, forward], axis=1).reshape(rows, wide).astype(jnp.bfloat16)
+            partner[lane, pair:] = crossed
+            partner[lane, :pair] = crossed[rows - pair :]
+
+    def correlate(lane, slot):
+        cos_a, cos_b, sine, scale = (slot_table[k, slot] for k in range(4))
+        left = last[lane, pair : rows + pair]
+        for row, right in enumerate((partner[lane, pair:], partner[lane, :rows])):
+            outer = lax.dot_general(left, right, (((0,), (0,)), ((), ())), preferred_element_type=jnp.float32)
+            outer = outer * scale
+            first, second = outer[:channels, :channels], outer[channels:, channels:]
+            total[row, 0] += first + second
+            total[row, 1] += cos_a * first + cos_b * second
+            total[row, 2] += sine * (outer[channels:, :channels] - outer[:channels, channels:])
+
+    early, late = (0, 1), (2, 3)
+    for lane in early:
+        weigh(lane, lane)
+    for lane in late:
+        last[lane] = jnp.zeros_like(last[lane])
+        partner[lane] = jnp.zeros_like(partner[lane])
+
     def slot_group(index, carry):
-        slots = [index * group + lane for lane in range(group)]
-        for lane, slot in enumerate(slots):
-            cos_a, cos_b, sine = slot_table[0, slot], slot_table[1, slot], slot_table[2, slot]
-            for row in range(3):
-                turned = (sine * mixes[row, 2]).astype(jnp.bfloat16)
-                lo, hi = row * wide, row * wide + channels
-                weights[lane, lo:hi, :channels] = (mixes[row, 0] + cos_a * mixes[row, 1]).astype(jnp.bfloat16)
-                weights[lane, hi : hi + channels, channels:] = (mixes[row, 0] + cos_b * mixes[row, 1]).astype(jnp.bfloat16)
-                weights[lane, lo:hi, channels:] = turned
-                weights[lane, hi : hi + channels, :channels] = -turned
-        powers = 2 ** (NS_STEPS + 1) - 1
-        for step in range(powers):
-            for lane, slot in enumerate(slots):
-                source = base.at[slot] if step == 0 else (state if step % 2 else other).at[lane]
-                target = (other if step % 2 else state).at[lane]
-                product = apply(source, weights[lane]).reshape(side, 2, images, wide)
-                start = base[slot, pair : rows + pair].astype(jnp.float32).reshape(side, 2, images, wide)
-                forward = start[:, 0] - product[:, 0]
-                backward = start[:, 1] + product[:, 1]
-                joined = jnp.stack([forward, backward], axis=1).reshape(rows, wide).astype(jnp.bfloat16)
-                target[pair : rows + pair] = joined
-                if step < powers - 1:
-                    target[:pair] = joined[rows - pair :]
-                    target[rows + pair :] = joined[:pair]
-                else:
-                    finished = (2.0 / GAIN**2) * forward - (1.0 / GAIN**2) * start[:, 0]
-                    answer[slot] = finished.reshape(side * images, wide)
-                    crossed = jnp.stack([-backward, forward], axis=1).reshape(rows, wide).astype(jnp.bfloat16)
-                    partner[lane, pair:] = crossed
-                    partner[lane, :pair] = crossed[rows - pair :]
-        last = state if powers % 2 else other
-        for lane, slot in enumerate(slots):
-            cos_a, cos_b, sine, scale = (slot_table[k, slot] for k in range(4))
-            left = last[lane, pair : rows + pair]
-            for row, right in enumerate((partner[lane, pair:], partner[lane, :rows])):
-                outer = lax.dot_general(left, right, (((0,), (0,)), ((), ())), preferred_element_type=jnp.float32)
-                outer = outer * scale
-                first, second = outer[:channels, :channels], outer[channels:, channels:]
-                total[row, 0] += first + second
-                total[row, 1] += cos_a * first + cos_b * second
-                total[row, 2] += sine * (outer[channels:, :channels] - outer[:channels, channels:])
+        slot = [index * group + lane for lane in range(group)]
+        before = [jnp.maximum(slot[lane] - group, 0) for lane in range(group)]
+        after = [jnp.minimum(slot[lane] + group, half - 1) for lane in range(group)]
+        for lane in early:
+            power(lane, slot[lane], 0)
+            correlate(lane + 2, before[lane + 2])
+        for step in range(1, powers - 1):
+            for lane in early:
+                power(lane, slot[lane], step)
+                if step == 2:
+                    weigh(lane + 2, slot[lane + 2])
+        for lane in early:
+            power(lane + 2, slot[lane + 2], 0)
+            power(lane, slot[lane], powers - 1)
+        for lane in early:
+            power(lane + 2, slot[lane + 2], 1)
+            correlate(lane, slot[lane])
+        for step in range(2, powers):
+            for lane in late:
+                power(lane, slot[lane], step)
+                if step == 3:
+                    weigh(lane - 2, after[lane - 2])
         return carry
 
     lax.fori_loop(0, half // group, slot_group, 0)
+    for lane in late:
+        correlate(lane, half - group + lane)
 
     def lay(place, piece):
         chunks[:, :, place] = piece.reshape(2, chips, channels)
@@ -191,25 +228,18 @@
     swap.wait()
     mine[...] = chunks[core] + from_partner[...]
 
-    def scatter(ahead, carry):
-        there = (chip + ahead) % chips
+    for ahead in far_first:
+        there = chip ^ ahead
         remote(mine.at[there], received.at[ahead - 1], chip_send.at[0], chip_recv.at[0], there, core).start()
-        return carry
-
-    lax.fori_loop(1, chips, scatter, 0)
     lax.fori_loop(third, 2 * third, synthesise, 0, unroll=True)
     everything = pltpu.make_async_copy(received, received, chip_recv.at[0])
     everything.wait()
     pltpu.make_async_copy(received, received, chip_send.at[0]).wait()
     gathered[core, chip] = mine[chip] + jnp.sum(received[...], axis=0)
 
-    def spread(ahead, carry):
-        there = (chip + ahead) % chips
-        piece = gathered.at[core, chip]
-        remote(piece, piece, chip_send.at[1], chip_recv.at[1], there, core).start()
-        return carry
-
-    lax.fori_loop(1, chips, spread, 0)
+    piece = gathered.at[core, chip]
+    for ahead in far_first:
+        remote(piece, piece, chip_send.at[1], chip_recv.at[1], chip ^ ahead, core).start()
     lax.fori_loop(2 * third, side // 2, synthesise, 0, unroll=True)
     store = pltpu.make_async_copy(result, outputs_hbm, out_sem)
     store.start()
@@ -228,7 +258,7 @@
     store.wait()
 
 
-def layer(pictures, cotangent, kernel, total_images, group=2):
+def layer(pictures, cotangent, kernel, total_images, group=4):
     images, side, _, channels = pictures.shape
     half = side // 2
     pair = 2 * images

time: 62.9 us -> 58.8 us (0.935)
  Pallas kernels: 57.9 us -> 53.9 us
    pallas_call x1, Pallas kernels: 57.9 us -> 53.9 us  [layer(): pl.pallas_call(functools.partial(layer_kernel, images, channels, side, gr...]
where the time goes in v3:
time: 58.8 us; the launch traced here: 58.7 us
  Pallas kernels  53.9 us (92%)
  local copies, waits for them, and re-layouts  4.15 us (7%)
  between operations  0.65 us (1%)
    pallas_call x1, Pallas kernels, layer(): pl.pallas_call(functools.partial(layer_kernel, images, channels, side, gr...  53.9 us
    unnamed x4, local copies, waits for them, and re-layouts  4.15 us

profile of v3, /device:TPU:1, one launch (start us, length us, event | category | flops | bytes accessed | tf_op | source)
XLA Modules:
  0.0 58.7 jit_solution(17015465319351625131)
XLA Ops:
  0.6 53.9 %layer.1 = (bf16[8,32,32,128]{3,2,1,0:T(8,128)(2,1)}, f32[3,3,128,128]{3,2,1,0:T(8,128)}) custom-call(f32[4,16]{1,0:T(4,128)} %constant.8.clone.slot_table, bf16[8,32,32,128]{3,2,1,0:T(8,128)(2,1)} %pictures_hbm.1, bf16[8,32,32,128]{3,2,1,0:T(8,128)(2,1)} %cotangent_hbm.1, f32[3,3,128,128]{3,2,1,0:T(8,128)} %taps_hbm.1, ...), custom_call_target="tpu_custom_call" | custom-call | tf_op jit(solution)/shard_map/layer/pallas_call | solution.py:273
  54.5 0.0 copy-start
  54.5 3.3 %copy.10 = bf16[8,32,32,128]{3,2,1,0:T(8,128)(2,1)} copy(bf16[8,32,32,128]{3,2,1,0:T(8,128)(2,1)} %get-tuple-element.4) | data formatting | bytes 4194304
  57.9 0.0 copy-done
  57.9 0.8 %copy.11 = f32[3,3,128,128]{3,2,1,0:T(8,128)} copy(f32[3,3,128,128]{3,2,1,0:T(8,128)S(1)} %copy-done) | data formatting | bytes 1179648
Async XLA Ops:
  54.5 3.3 %copy-start = (f32[3,3,128,128]{3,2,1,0:T(8,128)S(1)}, f32[3,3,128,128]{3,2,1,0:T(8,128)}, u32[]{:S(2)}) copy-start(f32[3,3,128,128]{3,2,1,0:T(8,128)} %get-tuple-element.5) | copy-start | bytes 1769476

commit v4 on v3

--- a/solution.py
+++ b/solution.py
@@ -48,9 +48,9 @@
 
 def layer_kernel(
     images, channels, side, group, slot_table, pictures_hbm, cotangent_hbm, taps_hbm, analysis_hbm, synthesis_hbm,
-    outputs_hbm, kernel_grad,
+    result, kernel_grad,
     pictures, cotangent, taps, analysis, synthesis, mixes, weights, base, state, other, partner, answer, total,
-    result, chunks, from_partner, mine, received, gathered, in_sem, out_sem, core_sem, chip_send, chip_recv,
+    chunks, from_partner, mine, received, gathered, in_sem, core_sem, chip_send, chip_recv,
 ):
     half = side // 2
     pair = 2 * images
@@ -241,8 +241,6 @@
     for ahead in far_first:
         remote(piece, piece, chip_send.at[1], chip_recv.at[1], chip ^ ahead, core).start()
     lax.fori_loop(2 * third, side // 2, synthesise, 0, unroll=True)
-    store = pltpu.make_async_copy(result, outputs_hbm, out_sem)
-    store.start()
     pltpu.make_async_copy(received, received, chip_recv.at[1]).wait()
     pltpu.make_async_copy(received, received, chip_send.at[1]).wait()
     ours = gathered.at[core]
@@ -255,7 +253,6 @@
         kernel_grad[row, col] = sums[place]
         if place:
             kernel_grad[2 - row, 2 - col] = -sums[place].T
-    store.wait()
 
 
 def layer(pictures, cotangent, kernel, total_images, group=4):
@@ -273,11 +270,11 @@
     return pl.pallas_call(
         functools.partial(layer_kernel, images, channels, side, group),
         out_shape=(
-            jax.ShapeDtypeStruct(pictures.shape, jnp.bfloat16),
-            jax.ShapeDtypeStruct(kernel.shape, jnp.float32),
+            pltpu.VMEM(pictures.shape, jnp.bfloat16),
+            pltpu.VMEM(kernel.shape, jnp.float32),
         ),
         in_specs=[pl.BlockSpec(memory_space=pltpu.SMEM)] + [anywhere] * 5,
-        out_specs=(anywhere, pl.BlockSpec(memory_space=pltpu.VMEM)),
+        out_specs=(pl.BlockSpec(memory_space=pltpu.VMEM), pl.BlockSpec(memory_space=pltpu.VMEM)),
         scratch_shapes=[
             pltpu.VMEM(pictures.shape, jnp.bfloat16),
             pltpu.VMEM(pictures.shape, jnp.bfloat16),
@@ -292,19 +289,17 @@
             pltpu.VMEM((group, rows + pair, wide), jnp.bfloat16),
             pltpu.VMEM((half, side * images, wide), jnp.float32),
             pltpu.VMEM((2, 3, channels, channels), jnp.float32),
-            pltpu.VMEM(pictures.shape, jnp.bfloat16),
             pltpu.VMEM((2, chips, 5, channels), jnp.float32),
             pltpu.VMEM((chips, 5, channels), jnp.float32),
             pltpu.VMEM((chips, 5, channels), jnp.float32),
             pltpu.VMEM((chips - 1, 5, channels), jnp.float32),
             pltpu.VMEM((2, chips, 5, channels), jnp.float32),
             pltpu.SemaphoreType.DMA((5,)),
-            pltpu.SemaphoreType.DMA,
             pltpu.SemaphoreType.DMA((4,)),
             pltpu.SemaphoreType.DMA((2,)),
             pltpu.SemaphoreType.DMA((2,)),
         ],
-        compiler_params=pltpu.CompilerParams(vmem_limit_bytes=63 * 1024 * 1024, collective_id=0, has_side_effects=True),
+        compiler_params=pltpu.CompilerParams(vmem_limit_bytes=60 * 1024 * 1024, collective_id=0, has_side_effects=True),
         name="layer",
     )(table, pictures, cotangent, kernel, analysis, synthesis)
 

time: 58.8 us -> 56 us (0.952)
  local copies, waits for them, and re-layouts: 4.15 us -> 2.14 us
  Pallas kernels: 53.9 us -> 53.1 us
    unnamed x4 -> x2, local copies, waits for them, and re-layouts: 4.15 us -> 2.14 us
    pallas_call x1, Pallas kernels: 53.9 us -> 53.1 us  [layer(): pl.pallas_call(functools.partial(layer_kernel, images, channels, side, gr...]
where the time goes in v4:
time: 56 us; the launch traced here: 55.8 us
  Pallas kernels  53.1 us (95%)
  local copies, waits for them, and re-layouts  2.14 us (4%)
  between operations  0.64 us (1%)
    pallas_call x1, Pallas kernels, layer(): pl.pallas_call(functools.partial(layer_kernel, images, channels, side, gr...  53.1 us
    unnamed x2, local copies, waits for them, and re-layouts  2.14 us

profile of v4, /device:TPU:1, one launch (start us, length us, event | category | flops | bytes accessed | tf_op | source)
XLA Modules:
  0.0 55.8 jit_solution(2807459437885591039)
XLA Ops:
  0.6 53.1 %layer.1 = (bf16[8,32,32,128]{3,2,1,0:T(8,128)(2,1)S(1)}, f32[3,3,128,128]{3,2,1,0:T(8,128)S(1)}) custom-call(f32[4,16]{1,0:T(4,128)} %constant.8.clone.slot_table, bf16[8,32,32,128]{3,2,1,0:T(8,128)(2,1)} %pictures_hbm.1, bf16[8,32,32,128]{3,2,1,0:T(8,128)(2,1)} %cotangent_hbm.1, f32[3,3,128,128]{3,2,1,0:T(8,128)} %taps_hbm.1, ...), custom_call_target="tpu_custom_call" | custom-call | tf_op jit(solution)/shard_map/layer/pallas_call | solution.py:270
  53.7 1.3 %copy.10 = bf16[8,32,32,128]{3,2,1,0:T(8,128)(2,1)} copy(bf16[8,32,32,128]{3,2,1,0:T(8,128)(2,1)S(1)} %get-tuple-element.2) | data formatting | bytes 4194304
  55.0 0.8 %copy.11 = f32[3,3,128,128]{3,2,1,0:T(8,128)} copy(f32[3,3,128,128]{3,2,1,0:T(8,128)S(1)} %get-tuple-element.3) | data formatting | bytes 1179648

commit v5 on v4

--- a/solution.py
+++ b/solution.py
@@ -82,6 +82,12 @@
     ]
     for load in loads:
         load.start()
+    def greet(beside, carry):
+        there = place_of(chip ^ beside, jnp.where(beside == 0, 1 - core, core))
+        pl.semaphore_signal(barrier, inc=1, device_id=there, device_id_type=pl.DeviceIdType.MESH)
+        return carry
+
+    lax.fori_loop(0, chips, greet, 0, unroll=8)
     loads[0].wait()
     for row in range(3):
         across = [taps[row, col].T - taps[2 - row, 2 - col] for col in range(3)]
@@ -90,12 +96,6 @@
         mixes[row, 2] = across[0] - across[2]
     total[...] = jnp.zeros_like(total)
 
-    def greet(beside, carry):
-        there = place_of(chip ^ beside, jnp.where(beside == 0, 1 - core, core))
-        pl.semaphore_signal(barrier, inc=1, device_id=there, device_id_type=pl.DeviceIdType.MESH)
-        return carry
-
-    lax.fori_loop(0, chips, greet, 0, unroll=8)
     for load in loads[1:4]:
         load.wait()
 
@@ -253,6 +253,31 @@
         kernel_grad[row, col] = sums[place]
         if place:
             kernel_grad[2 - row, 2 - col] = -sums[place].T
+
+
+def store_kernel(maps, gradient, maps_hbm, gradient_hbm, sems):
+    stores = [
+        pltpu.make_async_copy(maps, maps_hbm, sems.at[0]),
+        pltpu.make_async_copy(gradient, gradient_hbm, sems.at[1]),
+    ]
+    for store in stores:
+        store.start()
+    for store in stores:
+        store.wait()
+
+
+def store_both(maps, gradient):
+    inside = pl.BlockSpec(memory_space=pltpu.VMEM)
+    outside = pl.BlockSpec(memory_space=pltpu.HBM)
+    return pl.pallas_call(
+        store_kernel,
+        out_shape=(pltpu.HBM(maps.shape, maps.dtype), pltpu.HBM(gradient.shape, gradient.dtype)),
+        in_specs=[inside, inside],
+        out_specs=(outside, outside),
+        scratch_shapes=[pltpu.SemaphoreType.DMA((2,))],
+        compiler_params=pltpu.CompilerParams(vmem_limit_bytes=16 * 1024 * 1024),
+        name="store_both",
+    )(maps, gradient)
 
 
 def layer(pictures, cotangent, kernel, total_images, group=4):
@@ -306,7 +331,7 @@
 
 def per_device(images, cotangent, kernel):
     total = images.shape[0] * lax.axis_size("sample") * lax.axis_size("freq")
-    return layer(images, cotangent, kernel, total)
+    return store_both(*layer(images, cotangent, kernel, total))
 
 
 def solution(mesh):

time: 56 us -> 55.3 us (0.987)
  local copies, waits for them, and re-layouts: 2.14 us -> 0 us
  Pallas kernels: 53.1 us -> 54.6 us
    unnamed x2 -> x0, local copies, waits for them, and re-layouts: 2.14 us -> none
    pallas_call x0 -> x1, Pallas kernels: none -> 1.52 us  [store_both(): pl.pallas_call(store_kernel, out_shape=(pltpu.HBM(maps.shape, maps.dtype)...]
where the time goes in v5:
time: 55.3 us; the launch traced here: 55.2 us
  Pallas kernels  54.6 us (99%)
  between operations  0.64 us (1%)
    pallas_call x1, Pallas kernels, layer(): pl.pallas_call(functools.partial(layer_kernel, images, channels, side, gr...  53.1 us
    pallas_call x1, Pallas kernels, store_both(): pl.pallas_call(store_kernel, out_shape=(pltpu.HBM(maps.shape, maps.dtype)...  1.52 us

profile of v5, /device:TPU:1, one launch (start us, length us, event | category | flops | bytes accessed | tf_op | source)
XLA Modules:
  0.0 55.2 jit_solution(15140119655670502719)
XLA Ops:
  0.6 53.1 %layer.1 = (bf16[8,32,32,128]{3,2,1,0:T(8,128)(2,1)S(1)}, f32[3,3,128,128]{3,2,1,0:T(8,128)S(1)}) custom-call(f32[4,16]{1,0:T(4,128)} %constant.8.clone.slot_table, bf16[8,32,32,128]{3,2,1,0:T(8,128)(2,1)} %pictures_hbm.1, bf16[8,32,32,128]{3,2,1,0:T(8,128)(2,1)} %cotangent_hbm.1, f32[3,3,128,128]{3,2,1,0:T(8,128)} %taps_hbm.1, ...), custom_call_target="tpu_custom_call" | custom-call | tf_op jit(solution)/shard_map/layer/pallas_call | solution.py:295
  53.7 1.5 %store_both.1 = (bf16[8,32,32,128]{3,2,1,0:T(8,128)(2,1)}, f32[3,3,128,128]{3,2,1,0:T(8,128)}) custom-call(bf16[8,32,32,128]{3,2,1,0:T(8,128)(2,1)S(1)} %get-tuple-element.4.maps, f32[3,3,128,128]{3,2,1,0:T(8,128)S(1)} %get-tuple-element.5.gradient), custom_call_target="tpu_custom_call" | custom-call | tf_op jit(solution)/shard_map/store_both/pallas_call | solution.py:272
